TPU v7x, 256 devices: a whole 4x4x8 slice. The times are simulated.
256 devices in a mesh: frame: 8 (over x, y_lo), pos: 32 (over z, y_hi, core).
Axes of the slice: x: 4, y: 4 (y_hi: 2, y_lo: 2; y = y_hi * 2 + y_lo), z: 8, core: 2. Of those that a mesh axis runs over, the one named last changes fastest.
Arguments:
- frames_in: bfloat16 [512, 256, 512], P('frame', 'pos'), may hold values from -40 to 40
- attn_gain: float32 [512], replicated, may hold values from 0.5 to 1.5
- w_query: bfloat16 [512, 512], replicated, may hold values from -4 to 4
- w_key: bfloat16 [512, 512], replicated, may hold values from -4 to 4
- w_value: bfloat16 [512, 512], replicated, may hold values from -0.25 to 0.25
- w_output: bfloat16 [512, 512], replicated, may hold values from -0.25 to 0.25
- moe_gain: float32 [512], replicated, may hold values from 0.5 to 1.5
- dispatch_keys: bfloat16 [512, 1024], replicated, may hold values from -10 to 10
- w_in: bfloat16 [32, 512, 1024], P('pos'), may hold values from -0.25 to 0.25
- w_out: bfloat16 [32, 1024, 512], P('pos'), may hold values from -0.125 to 0.125
Outputs:
- frames_out: bfloat16 [512, 256, 512], P('frame', 'pos')
All inputs are finite; a program needn't handle non-finite values.
Results may differ from a plain program's by a relative error of at most 0.0052.
Values may be sent and summed in bfloat16 or wider, within the bound.
No kernel may reach another device: no remote copies, remote signals or barrier semaphores. Data moves between devices by JAX's collectives and lax.ppermute only.
A program may use at most 64 MiB of HBM per device.

v0:
```python
import jax
import jax.numpy as jnp
from jax import lax
from jax.sharding import PartitionSpec as P

HEADS = 8
EXPERTS = 16
SLOTS = 64
EPS = 1e-06
LOGIT_SCALE = 3.0
MASKED = -1e30


def copy_for_each(shard, axis):
    copies = jnp.broadcast_to(shard, (lax.axis_size(axis), *shard.shape))
    return lax.all_to_all(copies, axis, split_axis=0, concat_axis=0, tiled=True)


def collected_together(shard, axis):
    leaves = jax.tree.leaves(shard)
    sequence = sorted(range(len(leaves)), key=lambda k: -leaves[k].size)
    width = (1, *leaves[sequence[0]].shape)[-1]
    lines = [
        jnp.pad(leaves[k].reshape(-1), (0, -leaves[k].size % width)).reshape(-1, width)
        for k in sequence
    ]
    both, at, found = (copy_for_each(jnp.concatenate(lines), axis), 0, {})
    for k, line in zip(sequence, lines):
        piece = both[:, at : at + len(line)].reshape(len(both), -1)
        found[k] = piece[:, : leaves[k].size].reshape(-1, *leaves[k].shape)
        at += len(line)
    numbers = iter(range(len(leaves)))
    return jax.tree.map(lambda _: found[next(numbers)], shard)


def combined_pairwise(pieces, combine):
    while len(jax.tree.leaves(pieces)[0]) > 1:
        pieces = jax.vmap(combine)(
            *(jax.tree.map(lambda part: part[side::2], pieces) for side in (0, 1))
        )
    return jax.tree.map(lambda part: part[0], pieces)


def merged(shard, axis, combine):
    pieces = collected_together(shard, axis)
    return combined_pairwise(pieces, combine)


def in_blocks(shard, dim, length):
    before, after = (shard.shape[:dim], shard.shape[dim + 1 :])
    return jnp.moveaxis(shard.reshape(*before, length, -1, *after), dim, 0)


def sum_at_owner(shard, axis, dim):
    length = lax.axis_size(axis)
    blocks = lax.all_to_all(in_blocks(shard, dim, length), axis, 0, 0, tiled=True)
    return jnp.sum(blocks.astype(jnp.float32), axis=0)


def from_partner(block, axis, apart):
    count = lax.axis_size(axis)
    route = []
    for low in range(count):
        high = low | 1 << apart
        if high != low and high < count:
            route += [(low, high), (high, low)]
    return lax.ppermute(block, axis, route)


def in_order(blocks, dim):
    blocks = jnp.moveaxis(blocks, 0, dim)
    dims = blocks.shape
    return blocks.reshape(*dims[:dim], dims[dim] * dims[dim + 1], *dims[dim + 2 :])


def collect(shard, axis, dim):
    return in_order(copy_for_each(shard, axis), dim)


def rms_scale(values_in, gain):
    values_in = values_in.astype(jnp.float32)
    mean_sq = jnp.mean(values_in * values_in, axis=-1, keepdims=True)
    return values_in * lax.rsqrt(mean_sq + EPS) * gain


def project(rows_in, weights):
    return jnp.dot(rows_in, weights, preferred_element_type=jnp.float32).astype(jnp.bfloat16)


def softmax_rows(scores, axis_index):
    largest = jnp.max(scores, axis=axis_index, keepdims=True)
    weights = jnp.exp(scores - largest)
    return (weights / jnp.sum(weights, axis=axis_index, keepdims=True)).astype(jnp.bfloat16)


def attend(queries, keys_block, values_block):
    frame_count = queries.shape[0]
    score_scale = queries.shape[3] ** (-0.5)
    causal = jnp.arange(frame_count)[:, None] >= jnp.arange(frame_count)[None, :]

    def one_head(triple):
        queries_head, keys_head, values_head = triple
        scores = (
            jnp.einsum("fpd,gpd->pfg", queries_head, keys_head, preferred_element_type=jnp.float32)
            * score_scale
        )
        scores = jnp.where(causal[None], scores, MASKED)
        attention = softmax_rows(scores, 2)
        return jnp.einsum(
            "pfg,gpd->fpd", attention, values_head, preferred_element_type=jnp.float32
        ).astype(jnp.bfloat16)

    by_head = tuple(
        (jnp.moveaxis(array_in, 2, 0) for array_in in (queries, keys_block, values_block))
    )
    return jnp.moveaxis(lax.map(one_head, by_head), 0, 2)


def merge_stats(first_pair, second_pair):
    largest = jnp.maximum(first_pair[0], second_pair[0])
    totals = first_pair[1] * jnp.exp(first_pair[0] - largest) + second_pair[1] * jnp.exp(
        second_pair[0] - largest
    )
    return (largest, totals)


def local(
    frames_in, attn_gain, w_query, w_key, w_value, w_output, moe_gain, dispatch_keys, w_in, w_out
):
    frame_count, pos_count, features = frames_in.shape
    head_dim = features // HEADS
    normed = rms_scale(frames_in, attn_gain).astype(jnp.bfloat16)
    spread = lax.all_to_all(normed, "frame", split_axis=1, concat_axis=0, tiled=True)
    all_frames = spread.shape[0]
    pos_part = spread.shape[1]
    flattened = spread.reshape(all_frames * pos_part, features)
    shaped = (all_frames, pos_part, HEADS, head_dim)
    queries = project(flattened, w_query).reshape(shaped)
    keys_block = project(flattened, w_key).reshape(shaped)
    values_block = project(flattened, w_value).reshape(shaped)
    mixed_part = attend(queries, keys_block, values_block).reshape(all_frames, pos_part, features)
    mixed_heads = lax.all_to_all(mixed_part, "frame", split_axis=0, concat_axis=1, tiled=True)
    mixed_heads = mixed_heads.reshape(frame_count * pos_count, features)
    residual = (
        frames_in.reshape(frame_count * pos_count, features).astype(jnp.float32)
        + jnp.dot(mixed_heads, w_output, preferred_element_type=jnp.float32)
    ).astype(jnp.bfloat16)
    moe_input = rms_scale(residual, moe_gain).astype(jnp.bfloat16)
    logits = LOGIT_SCALE * jnp.dot(moe_input, dispatch_keys, preferred_element_type=jnp.float32)
    local_max = jnp.max(logits, axis=0)
    local_sum = jnp.sum(jnp.exp(logits - local_max[None, :]), axis=0)
    largest, totals = merged((local_max, local_sum), "pos", merge_stats)
    dispatch = (jnp.exp(logits - largest[None, :]) / totals[None, :]).astype(jnp.bfloat16)
    count_pos = lax.axis_size("pos")
    position = lax.axis_index("pos")
    splits = max(1, count_pos // EXPERTS)
    split_bits = splits.bit_length() - 1
    pieces_dev = EXPERTS * splits // count_pos
    local_experts = max(1, pieces_dev // splits)
    columns = dispatch
    slot_in = sum_at_owner(
        lax.dot_general(
            columns, moe_input, (((0,), (0,)), ((), ())), preferred_element_type=jnp.float32
        ).astype(jnp.bfloat16),
        "pos",
        0,
    ).astype(jnp.bfloat16)
    bit_index = 0
    partner = from_partner(slot_in, "pos", bit_index)
    upper_bit = position // 2**bit_index % 2 == 1
    slot_in = jnp.where(
        upper_bit,
        jnp.concatenate([partner, slot_in], axis=0),
        jnp.concatenate([slot_in, partner], axis=0),
    )
    slot_in = slot_in.reshape(local_experts, SLOTS, features)
    hidden = jax.nn.gelu(
        jnp.einsum("esd,edh->esh", slot_in, w_in, preferred_element_type=jnp.float32)
    ).astype(jnp.bfloat16)
    partial_out = jnp.einsum(
        "esh,ehd->esd", hidden, w_out, preferred_element_type=jnp.float32
    ).astype(jnp.bfloat16)
    shares = partial_out.astype(jnp.float32).reshape(pieces_dev * SLOTS, features)
    for bit_index in reversed(range(split_bits)):
        half_rows = shares.shape[0] // 2
        lower_half = shares[:half_rows]
        upper_half = shares[half_rows:]
        upper_bit = position // 2**bit_index % 2 == 1
        kept_rows = jnp.where(upper_bit, upper_half, lower_half)
        sent_rows = jnp.where(upper_bit, lower_half, upper_half)
        shares = kept_rows + from_partner(sent_rows.astype(jnp.bfloat16), "pos", bit_index).astype(
            sent_rows.dtype
        )
    outputs = shares.astype(jnp.bfloat16)
    combine = softmax_rows(logits, 1)
    columns = combine
    moe_out = jnp.dot(columns, collect(outputs, "pos", 0), preferred_element_type=jnp.float32)
    frames_out = (residual.astype(jnp.float32) + moe_out).astype(jnp.bfloat16)
    return frames_out.reshape(frame_count, pos_count, features)


def solution(mesh):
    in_specs = (
        P("frame", "pos", None),
        P(),
        P(),
        P(),
        P(),
        P(),
        P(),
        P(),
        P("pos", None, None),
        P("pos", None, None),
    )
    out_specs = P("frame", "pos", None)
    return jax.shard_map(local, mesh=mesh, in_specs=in_specs, out_specs=out_specs, check_vma=False)
```

profile of v0, /device:TPU:1, one launch (start us, length us, event | category | flops | bytes accessed | tf_op | source)
XLA Modules:
  0.0 160.5 jit_solution(891300015364039977)
XLA Ops:
  0.0 1.4 multiply_reduce_fusion
  1.5 2.1 %multiply_convert_fusion = bf16[64,8,512]{2,0,1:T(8,128)(2,1)} fusion(f32[512]{0:T(512)} %param.13, f32[64,8]{0,1:T(8,128)S(1)} %add_rsqrt_fusion, bf16[64,8,512]{2,1,0:T(8,128)(2,1)} %param.12), kind=kLoop, calls=%fused_computation.44 | loop fusion | flops 1048576 | bytes 1052672 | tf_op jit(solution)/shard_map/convert_element_type | solution.py:132
  3.5 6.0 %all-to-all-start = ((bf16[64,8,512]{2,0,1:T(8,128)(2,1)}), bf16[64,8,512]{2,0,1:T(8,128)(2,1)S(1)}, u32[]{:S(2)}, u32[]{:S(2)}) async-start(bf16[64,8,512]{2,0,1:T(8,128)(2,1)} %multiply_convert_fusion), calls=%async_computation | async-start | bytes 1048576 | tf_op jit(solution)/shard_map/all_to_all | solution.py:133
  9.5 8.7 %all-to-all-done = bf16[64,8,512]{2,0,1:T(8,128)(2,1)S(1)} async-done(((bf16[64,8,512]{2,0,1:T(8,128)(2,1)}), bf16[64,8,512]{2,0,1:T(8,128)(2,1)S(1)}, u32[]{:S(2)}, u32[]{:S(2)}) %all-to-all-start) | async-done | bytes 524320 | tf_op jit(solution)/shard_map/all_to_all | solution.py:133
  18.2 0.0 copy-done.5
  18.2 1.3 convolution_convert_fusion.3
  19.5 0.5 convolution_convert_fusion.2
  20.0 0.0 copy-done.7
  20.0 0.5 convolution_convert_fusion.4
  20.5 18.8 %while.11 = (s32[]{:T(128)}, bf16[8,512,1,64]{1,3,2,0:T(8,128)(2,1)}, bf16[8,512,1,64]{1,3,2,0:T(8,128)(2,1)S(1)}, bf16[8,512,1,64]{1,3,2,0:T(8,128)(2,1)}, bf16[8,512,1,64]{1,3,2,0:T(8,128)(2,1)S(1)}, /*index=5*/s32[]{:T(128)}) while((s32[]{:T(128)}, bf16[8,512,1,64]{1,3,2,0:T(8,128)(2,1)}, bf16[8,512,1,64]{1,3,2,0:T(8,128)(2,1)S(1)}, ...), condition=%wide.region_4.5_spmd.clone, body=%wide.region_1.4_spmd.clone.sunk | while | flops 69499904 | bytes 3420229 | solution.py:116
  20.5 1.2 fusion.86
  21.7 0.2 fusion.87
  21.9 0.9 fusion.88
  22.9 1.2 fusion.86
  24.1 0.2 fusion.87
  24.3 0.9 fusion.88
  25.2 1.2 fusion.86
  26.4 0.2 fusion.87
  26.6 0.9 fusion.88
  27.6 1.2 fusion.86
  28.8 0.2 fusion.87
  29.0 0.9 fusion.88
  29.9 1.2 fusion.86
  31.1 0.2 fusion.87
  31.3 1.0 fusion.88
  32.3 1.2 fusion.86
  33.5 0.2 fusion.87
  33.6 0.9 fusion.88
  34.6 1.2 fusion.86
  35.8 0.2 fusion.87
  36.0 0.9 fusion.88
  37.0 1.2 fusion.86
  38.2 0.2 fusion.87
  38.3 0.9 fusion.88
  39.3 0.5 broadcast.50
  39.8 2.0 %reduce.5 = bf16[512,512]{0,1:T(8,128)(2,1)S(1)} reduce(bf16[512,1,512]{0,2,1:T(8,128)(2,1)} %bitcast.117, bf16[]{:T(256)} %broadcast.50), dimensions={1}, to_apply=%copy.38.reduce_sub_computation | reduce | bytes 1048578 | tf_op jit(solution)/shard_map/reshape | solution.py:141
  41.9 0.2 copy.58
  42.1 1.2 reshape.156
  43.2 3.7 %all-to-all-start.1 = ((bf16[8,2,16384]{2,1,0:T(2,128)(2,1)}), bf16[8,2,16384]{2,1,0:T(2,128)(2,1)S(1)}, u32[]{:S(2)}, u32[]{:S(2)}) async-start(bf16[8,2,16384]{2,1,0:T(2,128)(2,1)} %reshape.156), calls=%async_computation.1 | async-start | bytes 1048576 | tf_op jit(solution)/shard_map/all_to_all | solution.py:142
  46.9 1.2 copy_convert_fusion
  48.1 6.9 %all-to-all-done.1 = bf16[8,2,16384]{2,1,0:T(2,128)(2,1)S(1)} async-done(((bf16[8,2,16384]{2,1,0:T(2,128)(2,1)}), bf16[8,2,16384]{2,1,0:T(2,128)(2,1)S(1)}, u32[]{:S(2)}, u32[]{:S(2)}) %all-to-all-start.1) | async-done | bytes 524320 | tf_op jit(solution)/shard_map/all_to_all | solution.py:142
  55.0 0.5 reshape.157
  55.6 0.0 copy-start.9
  55.6 0.1 copy.41
  55.7 2.2 %fusion.20 = (f32[512]{0:T(512)S(1)}, bf16[512,512]{1,0:T(8,128)(2,1)S(1)}) fusion(bf16[512,512]{1,0:T(8,128)(2,1)S(1)} %copy-done.8, bf16[64,8,1,512]{3,0,1,2:T(8,128)(2,1)S(1)} %bitcast.116, f32[64,8,512]{2,0,1:T(8,128)} %copy_convert_fusion), kind=kOutput, calls=%fused_computation.38 | convolution fusion | flops 269745664 | bytes 2623488 | tf_op jit(solution)/shard_map/dot_general | solution.py:146
  58.0 0.9 fusion.69
  58.9 0.7 fusion.14
  59.6 0.1 broadcast_in_dim.18
  59.7 26.0 %all_to_all.45 = f32[32,2,1024]{2,1,0:T(2,128)S(1)} all-to-all(f32[32,2,1024]{2,1,0:T(2,128)S(1)} %broadcast_in_dim.18), channel_id=1, replica_groups=mesh['frame'=8,'pos'=32] {'pos'}, dimensions={0} | all-to-all | bytes 524288 | tf_op jit(solution)/shard_map/all_to_all | solution.py:16
  85.7 0.2 fusion.71
  85.9 0.1 copy_bitcast_fusion
  86.5 1.9 %convolution_convert_fusion.1 = bf16[1024,512]{1,0:T(8,128)(2,1)S(1)} fusion(f32[512,1024]{1,0:T(8,128)S(1)} %get-tuple-element.80, f32[1024]{0:T(1024)S(1)} %bitcast.120, f32[1024]{0:T(1024)S(1)} %bitcast.121, bf16[512,512]{1,0:T(8,128)(2,1)} %copy-done.10, f32[512]{0:T(512)S(1)} %copy-done.9, f32[512]{0:T(512)S(1)} %add_rsqrt_fusion.1), kind=kOutput, calls=%fused_computation.27 | convolution fusion | flops 540016640 | bytes 3682304 | tf_op jit(solution)/shard_map/dot_general | solution.py:162
  88.4 0.0 copy-start.4
  88.4 32.1 %all_to_all.46 = bf16[32,32,512]{2,1,0:T(8,128)(2,1)S(1)} all-to-all(bf16[32,32,512]{2,1,0:T(8,128)(2,1)S(1)} %bitcast.112), channel_id=1, replica_groups=mesh['frame'=8,'pos'=32] {'pos'}, dimensions={0} | all-to-all | bytes 2097152 | tf_op jit(solution)/shard_map/all_to_all | solution.py:56
  120.6 0.2 reduce_sum.61
  120.7 0.8 collective-permute-start
  121.5 0.9 collective-permute-done
  122.4 1.7 %fusion.19 = f32[1,64,512]{2,1,0:T(8,128)S(1)} fusion(bf16[1,1024,512]{2,1,0:T(8,128)(2,1)S(1)} %copy-done.4, bf16[1,512,1024]{2,1,0:T(8,128)(2,1)} %param.20, bf16[32,512]{1,0:T(8,128)(2,1)S(1)} %reduce_sum.61, bf16[32,512]{1,0:T(8,128)(2,1)S(1)} %collective-permute-done, pred[]{:T(512)S(6)} %eq.7), kind=kOutput, calls=%fused_computation.37 | convolution fusion | flops 135168000 | bytes 2293761 | tf_op jit(solution)/shard_map/esh,ehd->esd/dot_general | solution.py:180
  124.2 0.0 copy-start.11
  124.2 0.4 collective-permute-start.1
  124.6 0.9 collective-permute-done.1
  125.5 0.1 broadcast_in_dim.19
  125.6 33.3 %all_to_all.47 = bf16[32,32,512]{2,1,0:T(8,128)(2,1)S(1)} all-to-all(bf16[32,32,512]{2,1,0:T(8,128)(2,1)S(1)} %broadcast_in_dim.19), channel_id=1, replica_groups=mesh['frame'=8,'pos'=32] {'pos'}, dimensions={0} | all-to-all | bytes 2097152 | tf_op jit(solution)/shard_map/all_to_all | solution.py:16
  158.9 1.6 fusion.17
  (46 shorter events, 0.6 us)
Async XLA Ops:
  0.0 58.0 %copy-start = (bf16[512,1024]{1,0:T(8,128)(2,1)S(1)}, bf16[512,1024]{1,0:T(8,128)(2,1)}, u32[]{:S(2)}) copy-start(bf16[512,1024]{1,0:T(8,128)(2,1)} %param.19) | copy-start | bytes 3145732
  0.0 18.2 %copy-start.5 = (bf16[512,512]{1,0:T(8,128)(2,1)S(1)}, bf16[512,512]{1,0:T(8,128)(2,1)}, u32[]{:S(2)}) copy-start(bf16[512,512]{1,0:T(8,128)(2,1)} %param.14) | copy-start | bytes 1572868
  0.0 19.5 %copy-start.6 = (bf16[512,512]{1,0:T(8,128)(2,1)S(1)}, bf16[512,512]{1,0:T(8,128)(2,1)}, u32[]{:S(2)}) copy-start(bf16[512,512]{1,0:T(8,128)(2,1)} %param.15) | copy-start | bytes 1572868
  3.5 16.5 %copy-start.7 = (bf16[512,512]{1,0:T(8,128)(2,1)S(1)}, bf16[512,512]{1,0:T(8,128)(2,1)}, u32[]{:S(2)}) copy-start(bf16[512,512]{1,0:T(8,128)(2,1)} %param.16) | copy-start | bytes 1572868
  3.5 14.7 %all-to-all-start = ((bf16[64,8,512]{2,0,1:T(8,128)(2,1)}), bf16[64,8,512]{2,0,1:T(8,128)(2,1)S(1)}, u32[]{:S(2)}, u32[]{:S(2)}) async-start(bf16[64,8,512]{2,0,1:T(8,128)(2,1)} %multiply_convert_fusion), calls=%async_computation | async-start | bytes 1048576 | tf_op jit(solution)/shard_map/all_to_all | solution.py:133
  39.8 7.1 %copy-start.1 = (bf16[64,8,512]{2,1,0:T(8,128)(2,1)S(1)}, bf16[64,8,512]{2,1,0:T(8,128)(2,1)}, u32[]{:S(2)}) copy-start(bf16[64,8,512]{2,1,0:T(8,128)(2,1)} %param.12) | copy-start | bytes 1572868
  43.2 11.8 %all-to-all-start.1 = ((bf16[8,2,16384]{2,1,0:T(2,128)(2,1)}), bf16[8,2,16384]{2,1,0:T(2,128)(2,1)S(1)}, u32[]{:S(2)}, u32[]{:S(2)}) async-start(bf16[8,2,16384]{2,1,0:T(2,128)(2,1)} %reshape.156), calls=%async_computation.1 | async-start | bytes 1048576 | tf_op jit(solution)/shard_map/all_to_all | solution.py:142
  48.1 7.6 %copy-start.8 = (bf16[512,512]{1,0:T(8,128)(2,1)S(1)}, bf16[512,512]{1,0:T(8,128)(2,1)}, u32[]{:S(2)}) copy-start(bf16[512,512]{1,0:T(8,128)(2,1)} %param.17) | copy-start | bytes 1572868
  55.6 2.4 %copy-start.9 = (f32[512]{0:T(512)S(1)}, f32[512]{0:T(512)}, u32[]{:S(2)}) copy-start(f32[512]{0:T(512)} %param.18) | copy-start | bytes 6148
  57.9 0.9 copy-start.10
  58.9 27.7 %copy-start.2 = (f32[512,1024]{1,0:T(8,128)}, f32[512,1024]{1,0:T(8,128)S(1)}, u32[]{:S(2)}) copy-start(f32[512,1024]{1,0:T(8,128)S(1)} %get-tuple-element.80) | copy-start | bytes 6291460
  88.4 34.0 %copy-start.4 = (bf16[1,1024,512]{2,1,0:T(8,128)(2,1)S(1)}, bf16[1,1024,512]{2,1,0:T(8,128)(2,1)}, u32[]{:S(2)}) copy-start(bf16[1,1024,512]{2,1,0:T(8,128)(2,1)} %param.21) | copy-start | bytes 3145732
  120.7 1.7 %collective-permute-start = (bf16[32,512]{1,0:T(8,128)(2,1)S(1)}, bf16[32,512]{1,0:T(8,128)(2,1)S(1)}, u32[]{:S(2)}, u32[]{:S(2)}) collective-permute-start(bf16[32,512]{1,0:T(8,128)(2,1)S(1)} %reduce_sum.61), channel_id=1, source_target_pairs={{0,1},{1,0},{2,3},{3,2},{4,5},{5,4},{6,7},{7,6},{8,9},{9,8},{10,11... | collective-permute-start | bytes 98312 | tf_op jit(solution)/shard_map/ppermute | solution.py:67
  124.1 34.8 %copy-start.3 = (f32[512,1024]{1,0:T(8,128)S(1)}, f32[512,1024]{1,0:T(8,128)}, u32[]{:S(2)}) copy-start(f32[512,1024]{1,0:T(8,128)} %copy-done.2) | copy-start | bytes 6291460
  124.2 34.8 %copy-start.11 = (bf16[512,512]{1,0:T(8,128)(2,1)S(1)}, bf16[512,512]{1,0:T(8,128)(2,1)}, u32[]{:S(2)}) copy-start(bf16[512,512]{1,0:T(8,128)(2,1)} %copy-done.10) | copy-start | bytes 1572868
  124.2 1.3 collective-permute-start.1
where the time goes:
time: 161 us
  blocking collectives  91.4 us (57%)
  matrix products  27.7 us (17%)
  waiting for transfers between devices  17.4 us (11%)
  starting transfers between devices  10.9 us (7%)
  other arithmetic  9.34 us (6%)
  local copies, waits for them, and re-layouts  3.4 us (2%)
    all_to_all x2, blocking collectives, copy_for_each(): return lax.all_to_all(copies, axis, split_axis=0, concat_axis=0, tiled=True)  59.3 us
    all_to_all x1, blocking collectives, sum_at_owner(): lax.all_to_all(in_blocks(shard, dim, length), axis, 0, 0, tiled=True)  32.1 us
    dot_general x8, matrix products, one_head(): jnp.einsum('fpd,gpd->pfg', queries_head, keys_head, preferred_element_typ...  9.6 us
    all_to_all x1, waiting for transfers between devices, local(): lax.all_to_all(normed, 'frame', split_axis=1, concat_axis=0, tiled=True)  8.71 us
    dot_general x8, matrix products, one_head(): jnp.einsum('pfg,gpd->fpd', attention, values_head, preferred_element_type...  7.6 us
    all_to_all x1, waiting for transfers between devices, local(): lax.all_to_all(mixed_part, 'frame', split_axis=0, concat_axis=1, tiled=True)  6.94 us
    all_to_all x1, starting transfers between devices, local(): lax.all_to_all(normed, 'frame', split_axis=1, concat_axis=0, tiled=True)  5.98 us
    all_to_all x1, starting transfers between devices, local(): lax.all_to_all(mixed_part, 'frame', split_axis=0, concat_axis=1, tiled=True)  3.67 us
  transfers between devices with their start and end apart: 4, of which 4 were waited for; matrix products, arithmetic and copies ran while one was open for 1% of the time, Pallas kernels for 0%

commit v1 on v0

--- a/solution.py
+++ b/solution.py
@@ -9,6 +9,15 @@
 EPS = 1e-06
 LOGIT_SCALE = 3.0
 MASKED = -1e30
+
+
+def define_slot(original):
+    return jnp.concatenate(
+        lax.all_to_all(
+            jnp.stack(jnp.split(original, lax.axis_size("frame"), 0), axis=0), "frame", 0, 0
+        ),
+        1,
+    )
 
 
 def copy_for_each(shard, axis):
@@ -139,7 +148,7 @@
     keys_block = project(flattened, w_key).reshape(shaped)
     values_block = project(flattened, w_value).reshape(shaped)
     mixed_part = attend(queries, keys_block, values_block).reshape(all_frames, pos_part, features)
-    mixed_heads = lax.all_to_all(mixed_part, "frame", split_axis=0, concat_axis=1, tiled=True)
+    mixed_heads = define_slot(mixed_part)
     mixed_heads = mixed_heads.reshape(frame_count * pos_count, features)
     residual = (
         frames_in.reshape(frame_count * pos_count, features).astype(jnp.float32)

time: 161 us -> 158 us (0.981)
  matrix products: 27.7 us -> 22.5 us
  local copies, waits for them, and re-layouts: 3.4 us -> 7.02 us
  other arithmetic: 9.34 us -> 6.32 us
    dot_general x8, matrix products: 7.6 us -> 2.5 us  [one_head(): jnp.einsum('pfg,gpd->fpd', attention, values_head, preferred_element_type...]
    unnamed x28 -> x29, local copies, waits for them, and re-layouts: 2.08 us -> 4.49 us
    reshape x1 -> x0, other arithmetic: 2.04 us -> none  [local(): attend(queries, keys_block, values_block)]
  transfers between devices with their start and end apart: 4 -> 4, of which waited for: 4 -> 4; matrix products, arithmetic and copies ran while one was open for 1% -> 0% of each run, Pallas kernels for 0% -> 0%
where the time goes in v1:
time: 158 us; the launch traced here: 157 us
  blocking collectives  91.4 us (58%)
  matrix products  22.5 us (14%)
  waiting for transfers between devices  18.3 us (12%)
  starting transfers between devices  10.8 us (7%)
  local copies, waits for them, and re-layouts  7.02 us (4%)
  other arithmetic  6.32 us (4%)
    all_to_all x2, blocking collectives, copy_for_each(): return lax.all_to_all(copies, axis, split_axis=0, concat_axis=0, tiled=True)  59.3 us
    all_to_all x1, blocking collectives, sum_at_owner(): lax.all_to_all(in_blocks(shard, dim, length), axis, 0, 0, tiled=True)  32.1 us
    dot_general x8, matrix products, one_head(): jnp.einsum('fpd,gpd->pfg', queries_head, keys_head, preferred_element_typ...  9.6 us
    all_to_all x1, waiting for transfers between devices, local(): lax.all_to_all(normed, 'frame', split_axis=1, concat_axis=0, tiled=True)  8.71 us
    all_to_all x1, waiting for transfers between devices, define_slot(): lax.all_to_all(jnp.stack(jnp.split(original, lax.axis_size('frame'), 0),...  7.92 us
    all_to_all x1, starting transfers between devices, local(): lax.all_to_all(normed, 'frame', split_axis=1, concat_axis=0, tiled=True)  5.85 us
    unnamed x29, local copies, waits for them, and re-layouts  4.49 us
    all_to_all x1, starting transfers between devices, define_slot(): lax.all_to_all(jnp.stack(jnp.split(original, lax.axis_size('frame'), 0),...  3.68 us
  transfers between devices with their start and end apart: 4, of which 4 were waited for; matrix products, arithmetic and copies ran while one was open for 0% of the time, Pallas kernels for 0%

profile of v1, /device:TPU:1, one launch (start us, length us, event | category | flops | bytes accessed | tf_op | source)
XLA Modules:
  0.0 156.8 jit_solution(13137158614427010459)
XLA Ops:
  0.0 1.4 multiply_reduce_fusion
  1.5 2.1 %multiply_convert_fusion = bf16[64,8,512]{2,0,1:T(8,128)(2,1)} fusion(f32[512]{0:T(512)} %param.13, f32[64,8]{0,1:T(8,128)S(1)} %add_rsqrt_fusion, bf16[64,8,512]{2,1,0:T(8,128)(2,1)} %param.12), kind=kLoop, calls=%fused_computation.44 | loop fusion | flops 1048576 | bytes 1052672 | tf_op jit(solution)/shard_map/convert_element_type | solution.py:141
  3.5 5.9 %all-to-all-start = ((bf16[64,8,512]{2,0,1:T(8,128)(2,1)}), bf16[64,8,512]{2,0,1:T(8,128)(2,1)S(1)}, u32[]{:S(2)}, u32[]{:S(2)}) async-start(bf16[64,8,512]{2,0,1:T(8,128)(2,1)} %multiply_convert_fusion), calls=%async_computation | async-start | bytes 1048576 | tf_op jit(solution)/shard_map/all_to_all | solution.py:142
  9.4 8.7 %all-to-all-done = bf16[64,8,512]{2,0,1:T(8,128)(2,1)S(1)} async-done(((bf16[64,8,512]{2,0,1:T(8,128)(2,1)}), bf16[64,8,512]{2,0,1:T(8,128)(2,1)S(1)}, u32[]{:S(2)}, u32[]{:S(2)}) %all-to-all-start) | async-done | bytes 524320 | tf_op jit(solution)/shard_map/all_to_all | solution.py:142
  18.1 1.3 convolution_convert_fusion.3
  19.4 0.5 convolution_convert_fusion.2
  19.9 0.5 convolution_convert_fusion.4
  20.4 13.8 %while.11 = (s32[]{:T(128)}, bf16[8,512,1,64]{1,3,2,0:T(8,128)(2,1)S(1)}, bf16[8,512,1,64]{1,3,2,0:T(8,128)(2,1)S(1)}, bf16[8,512,1,64]{1,3,2,0:T(8,128)(2,1)}, bf16[8,512,1,64]{1,3,2,0:T(8,128)(2,1)S(1)}, /*index=5*/s32[]{:T(128)}) while((s32[]{:T(128)}, bf16[8,512,1,64]{1,3,2,0:T(8,128)(2,1)S(1)}, ...), condition=%wide.region_4.5_spmd.clone, body=%wide.region_1.4_spmd.clone.sunk | while | flops 69499904 | bytes 3420229 | solution.py:125
  20.4 1.2 fusion.87
  21.6 0.2 fusion.88
  21.8 0.3 fusion.89
  22.1 1.2 fusion.87
  23.3 0.2 fusion.88
  23.5 0.3 fusion.89
  23.8 1.2 fusion.87
  25.0 0.2 fusion.88
  25.2 0.3 fusion.89
  25.6 1.2 fusion.87
  26.8 0.2 fusion.88
  27.0 0.3 fusion.89
  27.3 1.2 fusion.87
  28.5 0.2 fusion.88
  28.7 0.3 fusion.89
  29.0 1.2 fusion.87
  30.2 0.2 fusion.88
  30.4 0.3 fusion.89
  30.7 1.2 fusion.87
  31.9 0.2 fusion.88
  32.1 0.3 fusion.89
  32.5 1.2 fusion.87
  33.7 0.2 fusion.88
  33.9 0.3 fusion.89
  34.2 0.3 fusion.71
  34.5 0.1 copy.44
  34.6 0.6 constant_dynamic-update-slice_fusion.7
  35.5 0.1 copy.47
  35.7 0.1 copy.49
  35.9 0.1 copy.51
  36.0 0.6 constant_dynamic-update-slice_fusion.6
  36.6 0.6 constant_dynamic-update-slice_fusion.5
  37.3 0.6 constant_dynamic-update-slice_fusion.4
  37.9 0.6 constant_dynamic-update-slice_fusion.3
  38.5 0.6 constant_dynamic-update-slice_fusion.2
  39.2 0.6 constant_dynamic-update-slice_fusion.1
  39.8 0.6 constant_dynamic-update-slice_fusion
  40.4 3.7 %all-to-all-start.1 = ((bf16[8,64,1,512]{3,1,2,0:T(8,128)(2,1)}), bf16[8,64,1,512]{3,1,2,0:T(8,128)(2,1)S(1)}, u32[]{:S(2)}, u32[]{:S(2)}) async-start(bf16[8,64,1,512]{3,1,2,0:T(8,128)(2,1)} %constant_dynamic-update-slice_fusion), calls=%async_computation.1 | async-start | bytes 1048576 | tf_op jit(solution)/shard_map/all_to_all | solution.py:16
  44.1 0.2 copy_convert_fusion
  44.3 7.9 %all-to-all-done.1 = bf16[8,64,1,512]{3,1,2,0:T(8,128)(2,1)S(1)} async-done(((bf16[8,64,1,512]{3,1,2,0:T(8,128)(2,1)}), bf16[8,64,1,512]{3,1,2,0:T(8,128)(2,1)S(1)}, u32[]{:S(2)}, u32[]{:S(2)}) %all-to-all-start.1) | async-done | bytes 524320 | tf_op jit(solution)/shard_map/all_to_all | solution.py:16
  52.2 2.1 %fusion.20 = (f32[512]{0:T(512)S(1)}, bf16[512,512]{1,0:T(8,128)(2,1)S(1)}) fusion(bf16[512,512]{1,0:T(8,128)(2,1)} %param.17, bf16[64,8,1,512]{3,0,2,1:T(8,128)(2,1)S(1)} %bitcast.127, f32[64,8,512]{2,0,1:T(8,128)S(1)} %copy_convert_fusion), kind=kOutput, calls=%fused_computation.38 | convolution fusion | flops 269745664 | bytes 2623488 | tf_op jit(solution)/shard_map/dot_general | solution.py:155
  54.3 0.9 fusion.69
  55.2 0.7 fusion.14
  56.0 26.0 %all_to_all.35 = f32[32,2,1024]{2,1,0:T(2,128)S(1)} all-to-all(f32[32,2,1024]{2,1,0:T(2,128)S(1)} %broadcast_in_dim.18), channel_id=1, replica_groups=mesh['frame'=8,'pos'=32] {'pos'}, dimensions={0} | all-to-all | bytes 524288 | tf_op jit(solution)/shard_map/all_to_all | solution.py:25
  82.0 0.2 fusion.72
  82.9 1.9 %convolution_convert_fusion.1 = bf16[1024,512]{1,0:T(8,128)(2,1)S(1)} fusion(f32[512,1024]{1,0:T(8,128)S(1)} %get-tuple-element.88, f32[1024]{0:T(1024)S(1)} %bitcast.130, f32[1024]{0:T(1024)S(1)} %bitcast.131, bf16[512,512]{1,0:T(8,128)(2,1)} %copy-done.9, f32[512]{0:T(512)S(1)} %copy-done.8, f32[512]{0:T(512)S(1)} %add_rsqrt_fusion.1), kind=kOutput, calls=%fused_computation.27 | convolution fusion | flops 540016640 | bytes 3682304 | tf_op jit(solution)/shard_map/dot_general | solution.py:171
  84.8 32.1 %all_to_all.36 = bf16[32,32,512]{2,1,0:T(8,128)(2,1)S(1)} all-to-all(bf16[32,32,512]{2,1,0:T(8,128)(2,1)S(1)} %bitcast.115), channel_id=1, replica_groups=mesh['frame'=8,'pos'=32] {'pos'}, dimensions={0} | all-to-all | bytes 2097152 | tf_op jit(solution)/shard_map/all_to_all | solution.py:65
  116.9 0.2 reduce_sum.61
  117.0 0.8 collective-permute-start
  117.9 0.9 collective-permute-done
  118.7 1.7 %fusion.19 = f32[1,64,512]{2,1,0:T(8,128)S(1)} fusion(bf16[1,1024,512]{2,1,0:T(8,128)(2,1)S(1)} %copy-done.4, bf16[1,512,1024]{2,1,0:T(8,128)(2,1)} %param.20, bf16[32,512]{1,0:T(8,128)(2,1)S(1)} %reduce_sum.61, bf16[32,512]{1,0:T(8,128)(2,1)S(1)} %collective-permute-done, pred[]{:T(512)S(6)} %eq.7), kind=kOutput, calls=%fused_computation.37 | convolution fusion | flops 135168000 | bytes 2293761 | tf_op jit(solution)/shard_map/esh,ehd->esd/dot_general | solution.py:189
  120.5 0.4 collective-permute-start.1
  121.0 0.9 collective-permute-done.1
  121.8 0.1 broadcast_in_dim.19
  121.9 33.3 %all_to_all.37 = bf16[32,32,512]{2,1,0:T(8,128)(2,1)S(1)} all-to-all(bf16[32,32,512]{2,1,0:T(8,128)(2,1)S(1)} %broadcast_in_dim.19), channel_id=1, replica_groups=mesh['frame'=8,'pos'=32] {'pos'}, dimensions={0} | all-to-all | bytes 2097152 | tf_op jit(solution)/shard_map/all_to_all | solution.py:25
  155.3 1.6 %fusion.17 = bf16[64,8,512]{2,1,0:T(8,128)(2,1)} fusion(bf16[1024,512]{1,0:T(8,128)(2,1)S(1)} %bitcast.114, bf16[512,512]{1,0:T(8,128)(2,1)S(1)} %copy-done.10, f32[512,1024]{1,0:T(8,128)S(1)} %copy-done.3, f32[512]{0:T(512)S(1)} %get-tuple-element.50, f32[512]{0:T(512)S(1)} %get-tuple-element.52), kind=kOutput, calls=%fused_computation.34 | convolution fusion | flops 539230208 | bytes 4198400 | tf_op jit(solution)/shard_map/dot_general | solution.py:206
  (55 shorter events, 1.1 us)
Async XLA Ops:
  0.0 54.3 %copy-start = (bf16[512,1024]{1,0:T(8,128)(2,1)S(1)}, bf16[512,1024]{1,0:T(8,128)(2,1)}, u32[]{:S(2)}) copy-start(bf16[512,1024]{1,0:T(8,128)(2,1)} %param.19) | copy-start | bytes 3145732
  0.0 18.1 %copy-start.5 = (bf16[512,512]{1,0:T(8,128)(2,1)S(1)}, bf16[512,512]{1,0:T(8,128)(2,1)}, u32[]{:S(2)}) copy-start(bf16[512,512]{1,0:T(8,128)(2,1)} %param.14) | copy-start | bytes 1572868
  0.0 19.4 %copy-start.6 = (bf16[512,512]{1,0:T(8,128)(2,1)S(1)}, bf16[512,512]{1,0:T(8,128)(2,1)}, u32[]{:S(2)}) copy-start(bf16[512,512]{1,0:T(8,128)(2,1)} %param.15) | copy-start | bytes 1572868
  3.5 14.6 %all-to-all-start = ((bf16[64,8,512]{2,0,1:T(8,128)(2,1)}), bf16[64,8,512]{2,0,1:T(8,128)(2,1)S(1)}, u32[]{:S(2)}, u32[]{:S(2)}) async-start(bf16[64,8,512]{2,0,1:T(8,128)(2,1)} %multiply_convert_fusion), calls=%async_computation | async-start | bytes 1048576 | tf_op jit(solution)/shard_map/all_to_all | solution.py:142
  18.1 1.8 %copy-start.7 = (bf16[512,512]{1,0:T(8,128)(2,1)S(1)}, bf16[512,512]{1,0:T(8,128)(2,1)}, u32[]{:S(2)}) copy-start(bf16[512,512]{1,0:T(8,128)(2,1)} %param.16) | copy-start | bytes 1572868
  34.5 9.6 %copy-start.1 = (bf16[64,8,512]{2,1,0:T(8,128)(2,1)S(1)}, bf16[64,8,512]{2,1,0:T(8,128)(2,1)}, u32[]{:S(2)}) copy-start(bf16[64,8,512]{2,1,0:T(8,128)(2,1)} %param.12) | copy-start | bytes 1572868
  40.4 11.8 %all-to-all-start.1 = ((bf16[8,64,1,512]{3,1,2,0:T(8,128)(2,1)}), bf16[8,64,1,512]{3,1,2,0:T(8,128)(2,1)S(1)}, u32[]{:S(2)}, u32[]{:S(2)}) async-start(bf16[8,64,1,512]{3,1,2,0:T(8,128)(2,1)} %constant_dynamic-update-slice_fusion), calls=%async_computation.1 | async-start | bytes 1048576 | tf_op jit(solution)/shard_map/all_to_all | solution.py:16
  44.1 10.2 %copy-start.8 = (f32[512]{0:T(512)S(1)}, f32[512]{0:T(512)}, u32[]{:S(2)}) copy-start(f32[512]{0:T(512)} %param.18) | copy-start | bytes 6148
  54.3 0.9 copy-start.9
  55.2 27.7 %copy-start.2 = (f32[512,1024]{1,0:T(8,128)}, f32[512,1024]{1,0:T(8,128)S(1)}, u32[]{:S(2)}) copy-start(f32[512,1024]{1,0:T(8,128)S(1)} %get-tuple-element.88) | copy-start | bytes 6291460
  84.8 34.0 %copy-start.4 = (bf16[1,1024,512]{2,1,0:T(8,128)(2,1)S(1)}, bf16[1,1024,512]{2,1,0:T(8,128)(2,1)}, u32[]{:S(2)}) copy-start(bf16[1,1024,512]{2,1,0:T(8,128)(2,1)} %param.21) | copy-start | bytes 3145732
  117.0 1.7 %collective-permute-start = (bf16[32,512]{1,0:T(8,128)(2,1)S(1)}, bf16[32,512]{1,0:T(8,128)(2,1)S(1)}, u32[]{:S(2)}, u32[]{:S(2)}) collective-permute-start(bf16[32,512]{1,0:T(8,128)(2,1)S(1)} %reduce_sum.61), channel_id=1, source_target_pairs={{0,1},{1,0},{2,3},{3,2},{4,5},{5,4},{6,7},{7,6},{8,9},{9,8},{10,11... | collective-permute-start | bytes 98312 | tf_op jit(solution)/shard_map/ppermute | solution.py:76
  120.5 34.8 %copy-start.3 = (f32[512,1024]{1,0:T(8,128)S(1)}, f32[512,1024]{1,0:T(8,128)}, u32[]{:S(2)}) copy-start(f32[512,1024]{1,0:T(8,128)} %copy-done.2) | copy-start | bytes 6291460
  120.5 34.8 %copy-start.10 = (bf16[512,512]{1,0:T(8,128)(2,1)S(1)}, bf16[512,512]{1,0:T(8,128)(2,1)}, u32[]{:S(2)}) copy-start(bf16[512,512]{1,0:T(8,128)(2,1)} %copy-done.9) | copy-start | bytes 1572868
  120.5 1.3 collective-permute-start.1
